TPU v7x, 32 devices: a whole 2x2x4 slice. The times are simulated.
32 devices in a mesh: grp: 4 (over z), dev: 8 (over y, x, core).
Axes of the slice: x: 2, y: 2, z: 4, core: 2. Of those that a mesh axis runs over, the one named last changes fastest.
Arguments:
- positions: float32 [3, 128, 544], P(None, ('grp', 'dev')), may hold values from -2 to 20, as said below
- rest_shape: float32 [3, 544], replicated, may hold values from -3 to 3
- stiffness: float32 [544, 544], replicated, may hold values from -0.25 to 0.25
- up_map: float32 [544, 152], replicated, may hold values from -0.25 to 0.25
- down_map: float32 [152, 544], replicated, may hold values from -0.5 to 0.5
- m2m: float32 [152, 152], replicated, may hold values from -0.5 to 0.5
- box_template: float32 [3, 152], replicated, may hold values from -1 to 1
- near_target: int32 [32, 2], P(('grp', 'dev')), may hold values from 0 to 3
- near_owner: int32 [32, 2], P(('grp', 'dev')), may hold values from 0 to 7, as said below
- near_cell: int32 [32, 2], P(('grp', 'dev')), may hold values from 0 to 3, as said below
- near_count: int32 [32], P(('grp', 'dev')), may hold values from 1 to 2, as said below
Outputs:
- new_positions: float32 [3, 128, 544], P(None, ('grp', 'dev'))
- velocity: float32 [3, 128, 544], P(None, ('grp', 'dev'))
Inputs may be any that keep to these rules, and one draw needn't show every extreme that they name: `positions`: each cell's points lie within about 1.2 of the cell's center; devices of one group sit on a grid of spacing 2.5, groups are 6 apart. `near_owner`: device e's slots name devices of e's own group other than e itself; at most 2 used slots of one device name the same owner, and device 0 uses all 2 slots with exactly 2 on each owner it names. `near_cell`: the source cells named by one device's used slots are distinct. `near_count`: the used slots come first; device 0 uses all of them.
All inputs are finite; a program needn't handle non-finite values.
Results may differ from a plain program's by a relative error of at most 0.0003.
Values sent between devices are 32-bit elements; how exact they have to be, the bound alone decides.
No kernel may reach another device: no remote copies, remote signals or barrier semaphores. Data moves between devices by JAX's collectives and lax.ppermute only.
A program may use at most 64 MiB of HBM per device.

v0:
```python
import jax
import jax.numpy as jnp
from jax import lax
from jax.sharding import PartitionSpec as P

NEAR = 2
STEPS = 2
EPSILON_SQ = 0.25
VISCOSITY = 0.039788735772973836
TIME_STEP = 0.1
SKALAK_HARDEN = 2.0
CHECK_RADIUS = 1.0
DEVICE_RADIUS = 1.5
GROUP_RADIUS = 6.0


def stokes(targets, sources, forces):
    delta_x = targets[0][:, None] - sources[0][None, :]
    delta_y = targets[1][:, None] - sources[1][None, :]
    delta_z = targets[2][:, None] - sources[2][None, :]
    square = delta_x * delta_x + delta_y * delta_y + delta_z * delta_z
    inverse = 1.0 / ((square + EPSILON_SQ) * jnp.sqrt(square + EPSILON_SQ))
    direct = (square + 2.0 * EPSILON_SQ) * inverse
    projected = (
        delta_x * forces[0][None, :] + delta_y * forces[1][None, :] + delta_z * forces[2][None, :]
    ) * inverse
    result = jnp.einsum("ts,ks->kt", direct, forces, precision=lax.Precision.HIGHEST)
    extra = jnp.stack(
        [
            jnp.sum(delta_x * projected, axis=1),
            jnp.sum(delta_y * projected, axis=1),
            jnp.sum(delta_z * projected, axis=1),
        ]
    )
    return VISCOSITY * (result + extra)


def membrane(points, rest_shape, stiffness):
    centroid = jnp.mean(points, axis=2, keepdims=True)
    strain = points - centroid - rest_shape[:, None, :]
    linear = jnp.dot(
        strain.reshape(-1, strain.shape[2]), stiffness, precision=lax.Precision.HIGHEST
    ).reshape(strain.shape)
    stretch = jnp.sum(linear * linear, axis=0)
    return -linear * (1.0 + SKALAK_HARDEN * stretch / (1.0 + stretch))


def box_far(checks, equivalents, centers, radius, weights, box_template):
    sources = centers[:, :, None] + radius * box_template[None]
    forces = equivalents * weights.astype(equivalents.dtype)[:, None, None]
    source_count = equivalents.shape[0] * equivalents.shape[2]
    flat_sources = jnp.transpose(sources, (1, 0, 2)).reshape(3, source_count)
    flat_forces = jnp.transpose(forces, (1, 0, 2)).reshape(3, source_count)
    return stokes(checks, flat_sources, flat_forces)


def body(
    positions,
    rest_shape,
    stiffness,
    up_map,
    down_map,
    m2m,
    box_template,
    near_target,
    near_owner,
    near_cell,
    near_count,
):
    own_device = lax.axis_index("dev")
    own_group = lax.axis_index("grp")
    dev_count = lax.axis_size("dev")
    cell_count = positions.shape[1]
    slot_ids = jnp.arange(NEAR, dtype=jnp.int32)
    owners = near_owner[0]
    cell_ids = near_cell[0]
    targets = near_target[0]
    in_use = slot_ids < near_count[0]
    onehot = (
        (targets[:, None] == jnp.arange(cell_count, dtype=jnp.int32)[None, :]) & in_use[:, None]
    ).astype(jnp.float32)
    source_rows = owners * cell_count + cell_ids
    points = positions
    velocity = jnp.zeros_like(positions)
    for step_index in range(STEPS):
        forces = membrane(points, rest_shape, stiffness)
        stacked = jnp.concatenate([points, forces], axis=0)
        source_pool = lax.all_gather(stacked, "dev", axis=1, tiled=True)
        sources = jnp.take(source_pool, source_rows, axis=1)
        receivers = jnp.take(points, targets, axis=1)
        near_tiles = jax.vmap(stokes, in_axes=(1, 1, 1), out_axes=1)(
            receivers, sources[:3], sources[3:]
        )
        near_velocity = jnp.einsum(
            "ksp,sc->kcp", near_tiles, onehot, precision=lax.Precision.HIGHEST
        )
        equivalent = jnp.dot(jnp.sum(forces, axis=1), up_map, precision=lax.Precision.HIGHEST)
        center = jnp.mean(points, axis=(1, 2))
        checks = center[:, None] + CHECK_RADIUS * box_template
        box_forces = lax.all_gather(equivalent[None], "dev", axis=0, tiled=True)
        places = lax.all_gather(center[None], "dev", axis=0, tiled=True)
        indices = jnp.arange(box_forces.shape[0], dtype=jnp.int32)
        added = box_far(
            checks, box_forces, places, DEVICE_RADIUS, indices != own_device, box_template
        )
        equivalent_sum = jnp.sum(box_forces, axis=0)
        center_sum = jnp.sum(places, axis=0)
        group_eq = jnp.dot(equivalent_sum, m2m, precision=lax.Precision.HIGHEST)
        group_center = center_sum / dev_count
        outer_box_forces = lax.all_gather(group_eq[None], "grp", axis=0, tiled=True)
        outer_places = lax.all_gather(group_center[None], "grp", axis=0, tiled=True)
        outer_indices = jnp.arange(outer_box_forces.shape[0], dtype=jnp.int32)
        outer_far = box_far(
            checks,
            outer_box_forces,
            outer_places,
            GROUP_RADIUS,
            outer_indices != own_group,
            box_template,
        )
        far_checks = added + outer_far
        far_surface = jnp.dot(far_checks, down_map, precision=lax.Precision.HIGHEST)
        velocity = far_surface[:, None, :] + near_velocity
        points = points + TIME_STEP * velocity
    return (points, velocity)


def solution(mesh):
    return jax.shard_map(
        body,
        mesh=mesh,
        in_specs=(
            P(None, ("grp", "dev"), None),
            P(),
            P(),
            P(),
            P(),
            P(),
            P(),
            P(("grp", "dev"), None),
            P(("grp", "dev"), None),
            P(("grp", "dev"), None),
            P(("grp", "dev")),
        ),
        out_specs=(P(None, ("grp", "dev"), None), P(None, ("grp", "dev"), None)),
        check_vma=False,
    )
```

profile of v0, /device:TPU:0, one launch (start us, length us, event | category | flops | bytes accessed | tf_op | source)
XLA Modules:
  0.0 156.4 jit_solution(3233264386179120395)
XLA Ops:
  0.7 1.4 dynamic-slice
  2.7 0.9 fusion.199
  3.6 0.1 broadcast_multiply_fusion.5
  3.7 0.8 broadcast_multiply_fusion
  4.4 15.1 %all-reduce = f32[24]{0:T(128)S(1)} all-reduce(f32[24]{0:T(128)S(1)} %get-tuple-element.90), channel_id=3, replica_groups=mesh['grp'=4,'dev'=8] {'dev'}, use_global_device_ids=true, to_apply=%add | all-reduce | flops 24 | bytes 192
  20.1 1.6 %multiply_reduce_fusion.1 = (f32[4,544]{1,0:T(4,128)S(1)}, f32[3,4,544]{2,1,0:T(4,128)S(1)}) fusion(f32[544,544]{1,0:T(8,128)S(1)} %copy-done, f32[3,4,544]{2,1,0:T(4,128)} %param.15, f32[3,544]{1,0:T(4,128)} %param.16, f32[3,4]{1,0:T(4,128)S(1)} %broadcast_multiply_fusion.3), kind=kOutput, calls=%fused_computation.219 | convolution fusion | flops 42638720 | bytes 1251248 | tf_op jit(solution)/shard_map/dot_general | solution.py:41
  21.8 0.5 convolution_bitcast_fusion.1
  22.3 8.1 %all-gather.8 = f32[8,3,152]{2,1,0:T(4,128)S(1)} all-gather(f32[1,3,152]{2,1,0:T(4,128)S(1)} %convolution_bitcast_fusion.1), channel_id=2, replica_groups=mesh['grp'=4,'dev'=8] {'dev'}, dimensions={0}, use_global_device_ids=true | all-gather | bytes 16416 | tf_op jit(solution)/shard_map/all_gather | solution.py:100
  30.8 1.1 fusion.81
  31.9 0.1 reshape.201
  32.0 1.3 convolution_add_fusion.5
  33.4 0.6 dynamic-slice.1
  34.6 0.1 multiply_dynamic-update-slice_fusion.1
  34.7 11.9 %all-reduce.1 = f32[12]{0:T(128)S(1)} all-reduce(f32[12]{0:T(128)S(1)} %multiply_dynamic-update-slice_fusion.1), channel_id=5, replica_groups=mesh['grp'=4,'dev'=8] {'grp'}, use_global_device_ids=true, to_apply=%add.1 | all-reduce | flops 12 | bytes 96
  46.7 0.1 copy.44
  47.1 0.2 convolution_bitcast_fusion.3
  47.3 13.2 %all-gather.9 = f32[4,3,152]{2,1,0:T(4,128)S(1)} all-gather(f32[1,3,152]{2,1,0:T(4,128)S(1)} %convolution_bitcast_fusion.3), channel_id=4, replica_groups=mesh['grp'=4,'dev'=8] {'grp'}, dimensions={0}, use_global_device_ids=true | all-gather | bytes 9120 | tf_op jit(solution)/shard_map/all_gather | solution.py:110
  60.9 0.7 fusion.107
  61.7 0.1 reshape.202
  61.8 0.8 fusion.73
  62.6 0.3 fusion.213
  63.0 10.3 %all_gather.34 = f32[6,32,544]{2,0,1:T(8,128)S(1)} all-gather(f32[6,4,544]{2,0,1:T(8,128)S(1)} %copy.45), channel_id=1, replica_groups=mesh['grp'=4,'dev'=8] {'dev'}, dimensions={1}, use_global_device_ids=true | all-gather | bytes 470016 | tf_op jit(solution)/shard_map/all_gather | solution.py:88
  73.3 0.6 gather_fusion
  74.1 0.6 gather_fusion.1
  74.8 4.4 %fusion.7 = (f32[2,544]{1,0:T(2,128)S(1)}, f32[2,544]{1,0:T(2,128)S(1)}, f32[2,544]{1,0:T(2,128)S(1)}) fusion(f32[2,544]{1,0:T(2,128)S(1)} %get-tuple-element.103, f32[2,544]{1,0:T(2,128)S(1)} %get-tuple-element.69, f32[2,544]{1,0:T(2,128)S(1)} %get-tuple-element.98, f32[2,544]{1,0:T(2,128)S(1)} %get-tuple-element.101, f32[2,544]{1,0:T(2,128)S(1)} %get-tuple-element.70, ...), kind=kLoop, calls=%fused_computation.31 | loop fusion | flops 13609792 | bytes 52224 | tf_op jit(solution)/shard_map/vmap()/reduce_sum | solution.py:30
  79.2 4.6 %fusion.67 = f32[3,2,544]{2,0,1:T(4,128)S(1)} fusion(f32[2,544]{1,0:T(2,128)S(1)} %get-tuple-element.101, f32[2,544]{1,0:T(2,128)S(1)} %get-tuple-element.70, f32[2,544]{1,0:T(2,128)S(1)} %get-tuple-element.102, f32[2,544]{1,0:T(2,128)S(1)} %get-tuple-element.71, f32[2,544]{1,0:T(2,128)S(1)} %get-tuple-element.103, f32[2,544]{1,0:T(2,128)S(1)} %get-tuple-element.69, ...), kind=kOutput, calls=%fused_computation.99 | convolution fusion | flops 29014784 | bytes 79616 | tf_op jit(solution)/shard_map/vmap(ts,ks->kt)/dot_general | solution.py:27
  84.5 0.4 fusion.198
  84.9 0.9 multiply_reduce_fusion
  85.9 0.5 convolution_bitcast_fusion
  86.3 8.1 %all-gather.10 = f32[8,3,152]{2,1,0:T(4,128)S(1)} all-gather(f32[1,3,152]{2,1,0:T(4,128)S(1)} %convolution_bitcast_fusion), channel_id=6, replica_groups=mesh['grp'=4,'dev'=8] {'dev'}, dimensions={0}, use_global_device_ids=true | all-gather | bytes 16416 | tf_op jit(solution)/shard_map/all_gather | solution.py:100
  94.5 0.2 convolution_bitcast_fusion.2
  94.7 13.2 %all-gather.11 = f32[4,3,152]{2,1,0:T(4,128)S(1)} all-gather(f32[1,3,152]{2,1,0:T(4,128)S(1)} %convolution_bitcast_fusion.2), channel_id=8, replica_groups=mesh['grp'=4,'dev'=8] {'grp'}, dimensions={0}, use_global_device_ids=true | all-gather | bytes 9120 | tf_op jit(solution)/shard_map/all_gather | solution.py:110
  108.4 11.8 %all-reduce.2 = f32[24]{0:T(128)S(1)} all-reduce(f32[24]{0:T(128)S(1)} %get-tuple-element.88), channel_id=7, replica_groups=mesh['grp'=4,'dev'=8] {'dev'}, use_global_device_ids=true, to_apply=%add.2 | all-reduce | flops 24 | bytes 192
  120.3 0.1 multiply_dynamic-update-slice_fusion
  120.4 8.6 %all-reduce.3 = f32[12]{0:T(128)S(1)} all-reduce(f32[12]{0:T(128)S(1)} %multiply_dynamic-update-slice_fusion), channel_id=9, replica_groups=mesh['grp'=4,'dev'=8] {'grp'}, use_global_device_ids=true, to_apply=%add.3 | all-reduce | flops 12 | bytes 96
  129.0 0.1 copy.50
  129.5 0.7 fusion.118
  131.0 1.1 fusion.92
  132.1 0.1 reshape.203
  132.2 1.3 convolution_add_fusion.4
  133.6 0.8 fusion.71
  134.4 0.3 fusion.214
  134.8 10.1 %all_gather.39 = f32[6,32,544]{2,0,1:T(8,128)S(1)} all-gather(f32[6,4,544]{2,0,1:T(8,128)S(1)} %copy.51), channel_id=1, replica_groups=mesh['grp'=4,'dev'=8] {'dev'}, dimensions={1}, use_global_device_ids=true | all-gather | bytes 470016 | tf_op jit(solution)/shard_map/all_gather | solution.py:88
  145.0 0.5 gather_fusion.2
  145.7 0.6 gather_fusion.3
  146.4 4.4 %fusion.18 = (f32[2,544]{1,0:T(2,128)S(1)}, f32[2,544]{1,0:T(2,128)S(1)}, f32[2,544]{1,0:T(2,128)S(1)}) fusion(f32[2,544]{1,0:T(2,128)S(1)} %bitcast.162, f32[2,544]{1,0:T(2,128)S(1)} %bitcast.171, f32[2,544]{1,0:T(2,128)S(1)} %bitcast.164, f32[2,544]{1,0:T(2,128)S(1)} %bitcast.158, f32[2,544]{1,0:T(2,128)S(1)} %bitcast.167, f32[2,544]{1,0:T(2,128)S(1)} %bitcast.165, ...), kind=kLoop, calls=%fused_computation.42 | loop fusion | flops 13609792 | bytes 52224 | tf_op jit(solution)/shard_map/vmap()/reduce_sum | solution.py:30
  150.9 4.6 %fusion.61 = f32[3,2,544]{2,0,1:T(4,128)S(1)} fusion(f32[2,544]{1,0:T(2,128)S(1)} %bitcast.159, f32[2,544]{1,0:T(2,128)S(1)} %bitcast.168, f32[2,544]{1,0:T(2,128)S(1)} %bitcast.161, f32[2,544]{1,0:T(2,128)S(1)} %bitcast.170, f32[2,544]{1,0:T(2,128)S(1)} %bitcast.163, f32[2,544]{1,0:T(2,128)S(1)} %bitcast.172, f32[6,2,544]{2,0,1:T(8,128)S(1)} %select_bitcast_fusion, ...), kind=kOutput, calls=%fused_computation.97 | convolution fusion | flops 29014784 | bytes 79616 | tf_op jit(solution)/shard_map/vmap(ts,ks->kt)/dot_general | solution.py:27
  155.4 0.9 multiply_add_fusion
  (128 shorter events, 4.4 us)
Async XLA Ops:
  0.6 19.5 %copy-start = (f32[544,544]{1,0:T(8,128)S(1)}, f32[544,544]{1,0:T(8,128)}, u32[]{:S(2)}) copy-start(f32[544,544]{1,0:T(8,128)} %param.17) | copy-start | bytes 3551236
  0.6 21.1 %copy-start.1 = (f32[544,152]{0,1:T(8,128)S(1)}, f32[544,152]{0,1:T(8,128)}, u32[]{:S(2)}) copy-start(f32[544,152]{0,1:T(8,128)} %param.18) | copy-start | bytes 992260
  32.0 1.3 copy-start.10
  32.0 15.1 %copy-start.4 = (f32[152,152]{1,0:T(8,128)S(1)}, f32[152,152]{1,0:T(8,128)}, u32[]{:S(2)}) copy-start(f32[152,152]{1,0:T(8,128)} %param.20) | copy-start | bytes 277252
  60.9 1.7 %copy-start.2 = (f32[152,544]{1,0:T(8,128)S(1)}, f32[152,544]{1,0:T(8,128)}, u32[]{:S(2)}) copy-start(f32[152,544]{1,0:T(8,128)} %param.19) | copy-start | bytes 992260
  61.7 1.2 copy-start.3
  61.8 11.6 %copy-start.7 = (s32[1,2]{1,0:T(1,128)S(1)}, s32[1,2]{1,0:T(1,128)}, u32[]{:S(2)}) copy-start(s32[1,2]{1,0:T(1,128)} %param.24) | copy-start | bytes 28
  61.8 11.5 %copy-start.8 = (s32[1,2]{1,0:T(1,128)S(1)}, s32[1,2]{1,0:T(1,128)}, u32[]{:S(2)}) copy-start(s32[1,2]{1,0:T(1,128)} %param.23) | copy-start | bytes 28
  62.6 11.4 %copy-start.9 = (s32[1,2]{1,0:T(1,128)S(1)}, s32[1,2]{1,0:T(1,128)}, u32[]{:S(2)}) copy-start(s32[1,2]{1,0:T(1,128)} %param.22) | copy-start | bytes 28
  79.2 5.7 %copy-start.5 = (f32[3,544]{1,0:T(4,128)S(1)}, f32[3,544]{1,0:T(4,128)}, u32[]{:S(2)}) copy-start(f32[3,544]{1,0:T(4,128)} %param.16) | copy-start | bytes 19588
  83.8 45.6 %copy-start.6 = (f32[3,152]{1,0:T(4,128)S(1)}, f32[3,152]{1,0:T(4,128)}, u32[]{:S(2)}) copy-start(f32[3,152]{1,0:T(4,128)} %param.21) | copy-start | bytes 5476
where the time goes:
time: 157 us; the launch traced here: 156 us
  blocking collectives  111 us (71%)
  matrix products  19.1 us (12%)
  other arithmetic  15.7 us (10%)
  local copies, waits for them, and re-layouts  7.79 us (5%)
  between operations  3.27 us (2%)
    unnamed x4, blocking collectives  47.4 us
    all_gather x2, blocking collectives, body(): outer_box_forces = lax.all_gather(group_eq[None], 'grp', axis=0, tiled=True)  26.5 us
    all_gather x2, blocking collectives, body(): source_pool = lax.all_gather(stacked, 'dev', axis=1, tiled=True)  20.4 us
    all_gather x2, blocking collectives, body(): box_forces = lax.all_gather(equivalent[None], 'dev', axis=0, tiled=True)  16.2 us
    dot_general x6, matrix products, stokes(): jnp.einsum('ts,ks->kt', direct, forces, precision=lax.Precision.HIGHEST)  13.4 us
    reduce_sum x6, other arithmetic, stokes(): jnp.sum(delta_x * projected, axis=1)  12.5 us

commit v1 on v0

--- a/solution.py
+++ b/solution.py
@@ -12,6 +12,19 @@
 CHECK_RADIUS = 1.0
 DEVICE_RADIUS = 1.5
 GROUP_RADIUS = 6.0
+
+
+def ring_gather(shard, axis, dim):
+    size, index, width = (lax.axis_size(axis), lax.axis_index(axis), shard.shape[dim])
+    right = [(i, (i + 1) % size) for i in range(size)]
+    out = jnp.zeros((*shard.shape[:dim], size * width, *shard.shape[dim + 1 :]), shard.dtype)
+    current = shard
+    for step in range(size):
+        owner = (index - step) % size
+        out = lax.dynamic_update_slice_in_dim(out, current, owner * width, axis=dim)
+        if step < size - 1:
+            current = lax.ppermute(current, axis, right)
+    return out
 
 
 def stokes(targets, sources, forces):
@@ -107,7 +120,7 @@
         center_sum = jnp.sum(places, axis=0)
         group_eq = jnp.dot(equivalent_sum, m2m, precision=lax.Precision.HIGHEST)
         group_center = center_sum / dev_count
-        outer_box_forces = lax.all_gather(group_eq[None], "grp", axis=0, tiled=True)
+        outer_box_forces = ring_gather(group_eq[None], "grp", 0)
         outer_places = lax.all_gather(group_center[None], "grp", axis=0, tiled=True)
         outer_indices = jnp.arange(outer_box_forces.shape[0], dtype=jnp.int32)
         outer_far = box_far(

time: 157 us -> 156 us (level)
  blocking collectives: 111 us -> 87.8 us
  waiting for transfers between devices: 0 us -> 20.6 us
  starting transfers between devices: 0 us -> 1.67 us
    all_gather x2 -> x0, blocking collectives: 26.5 us -> none  [body(): outer_box_forces = lax.all_gather(group_eq[None], 'grp', axis=0, tiled=True)]
    ppermute x0 -> x6, waiting for transfers between devices: none -> 20.6 us  [ring_gather(): current = lax.ppermute(current, axis, right)]
    all_gather x2, blocking collectives: 16.2 us -> 18.7 us  [body(): box_forces = lax.all_gather(equivalent[None], 'dev', axis=0, tiled=True)]
    ppermute x0 -> x6, starting transfers between devices: none -> 1.67 us  [ring_gather(): current = lax.ppermute(current, axis, right)]
  transfers between devices with their start and end apart: 0 -> 6, of which waited for: 0 -> 4; matrix products, arithmetic and copies ran while one was open for 0% -> 20% of each run, Pallas kernels for 0% -> 0%
where the time goes in v1:
time: 156 us
  blocking collectives  87.8 us (56%)
  waiting for transfers between devices  20.6 us (13%)
  matrix products  19.1 us (12%)
  other arithmetic  15.4 us (10%)
  local copies, waits for them, and re-layouts  8.05 us (5%)
  between operations  3.4 us (2%)
  starting transfers between devices  1.67 us (1%)
    unnamed x4, blocking collectives  48.6 us
    ppermute x6, waiting for transfers between devices, ring_gather(): current = lax.ppermute(current, axis, right)  20.6 us
    all_gather x2, blocking collectives, body(): source_pool = lax.all_gather(stacked, 'dev', axis=1, tiled=True)  20.4 us
    all_gather x2, blocking collectives, body(): box_forces = lax.all_gather(equivalent[None], 'dev', axis=0, tiled=True)  18.7 us
    dot_general x6, matrix products, stokes(): jnp.einsum('ts,ks->kt', direct, forces, precision=lax.Precision.HIGHEST)  13.4 us
    reduce_sum x6, other arithmetic, stokes(): jnp.sum(delta_x * projected, axis=1)  12.5 us
  transfers between devices with their start and end apart: 6, of which 4 were waited for; matrix products, arithmetic and copies ran while one was open for 20% of the time, Pallas kernels for 0%

profile of v1, /device:TPU:0, one launch (start us, length us, event | category | flops | bytes accessed | tf_op | source)
XLA Modules:
  0.0 155.9 jit_solution(7812082428362876529)
XLA Ops:
  0.7 1.0 fusion.199
  1.7 0.5 copy-done
  2.2 1.6 %multiply_reduce_fusion.1 = (f32[4,544]{1,0:T(4,128)S(1)}, f32[3,4,544]{2,1,0:T(4,128)S(1)}) fusion(f32[544,544]{1,0:T(8,128)S(1)} %copy-done, f32[3,4,544]{2,1,0:T(4,128)} %param.15, f32[3,544]{1,0:T(4,128)} %param.16, f32[3,4]{1,0:T(4,128)S(1)} %broadcast_multiply_fusion.3), kind=kOutput, calls=%fused_computation.219 | convolution fusion | flops 42638720 | bytes 1251248 | tf_op jit(solution)/shard_map/dot_general | solution.py:54
  3.9 0.5 convolution_bitcast_fusion.1
  4.4 10.6 %all-gather.6 = f32[8,3,152]{2,1,0:T(4,128)S(1)} all-gather(f32[1,3,152]{2,1,0:T(4,128)S(1)} %convolution_bitcast_fusion.1), channel_id=2, replica_groups=mesh['grp'=4,'dev'=8] {'dev'}, dimensions={0}, use_global_device_ids=true | all-gather | bytes 16416 | tf_op jit(solution)/shard_map/all_gather | solution.py:113
  15.1 0.2 convolution_bitcast_fusion.3
  15.2 1.6 %collective-permute-start = (f32[1,3,152]{2,1,0:T(4,128)S(1)}, f32[1,3,152]{2,1,0:T(4,128)S(1)}, u32[]{:S(2)}, u32[]{:S(2)}) collective-permute-start(f32[1,3,152]{2,1,0:T(4,128)S(1)} %convolution_bitcast_fusion.3), channel_id=1, source_target_pairs={{0,8},{8,16},{16,24},{24,0},{1,9},{9,17},{17,25},{25,1},{2,10},{10... | collective-permute-start | bytes 5480 | tf_op jit(solution)/shard_map/ppermute | solution.py:26
  16.9 0.6 dynamic-slice
  18.1 0.1 broadcast_multiply_fusion.5
  18.2 12.9 %all-reduce = f32[24]{0:T(128)S(1)} all-reduce(f32[24]{0:T(128)S(1)} %get-tuple-element.90), channel_id=3, replica_groups=mesh['grp'=4,'dev'=8] {'dev'}, use_global_device_ids=true, to_apply=%add | all-reduce | flops 24 | bytes 192
  31.2 0.6 dynamic-slice.1
  32.6 0.1 multiply_dynamic-update-slice_fusion.1
  32.7 10.7 %all-reduce.1 = f32[12]{0:T(128)S(1)} all-reduce(f32[12]{0:T(128)S(1)} %multiply_dynamic-update-slice_fusion.1), channel_id=4, replica_groups=mesh['grp'=4,'dev'=8] {'grp'}, use_global_device_ids=true, to_apply=%add.1 | all-reduce | flops 12 | bytes 96
  44.5 10.3 %all_gather.27 = f32[6,32,544]{2,0,1:T(8,128)S(1)} all-gather(f32[6,4,544]{2,0,1:T(8,128)S(1)} %copy.60), channel_id=1, replica_groups=mesh['grp'=4,'dev'=8] {'dev'}, dimensions={1}, use_global_device_ids=true | all-gather | bytes 470016 | tf_op jit(solution)/shard_map/all_gather | solution.py:101
  54.9 0.6 gather_fusion
  55.5 0.6 gather_fusion.1
  56.3 4.4 %fusion.7 = (f32[2,544]{1,0:T(2,128)S(1)}, f32[2,544]{1,0:T(2,128)S(1)}, f32[2,544]{1,0:T(2,128)S(1)}) fusion(f32[2,544]{1,0:T(2,128)S(1)} %get-tuple-element.103, f32[2,544]{1,0:T(2,128)S(1)} %get-tuple-element.63, f32[2,544]{1,0:T(2,128)S(1)} %get-tuple-element.98, f32[2,544]{1,0:T(2,128)S(1)} %get-tuple-element.101, f32[2,544]{1,0:T(2,128)S(1)} %get-tuple-element.64, ...), kind=kLoop, calls=%fused_computation.31 | loop fusion | flops 13609792 | bytes 52224 | tf_op jit(solution)/shard_map/vmap()/reduce_sum | solution.py:43
  61.4 4.6 %fusion.67 = f32[3,2,544]{2,0,1:T(4,128)S(1)} fusion(f32[2,544]{1,0:T(2,128)S(1)} %get-tuple-element.101, f32[2,544]{1,0:T(2,128)S(1)} %get-tuple-element.64, f32[2,544]{1,0:T(2,128)S(1)} %get-tuple-element.102, f32[2,544]{1,0:T(2,128)S(1)} %get-tuple-element.65, f32[2,544]{1,0:T(2,128)S(1)} %get-tuple-element.103, f32[2,544]{1,0:T(2,128)S(1)} %get-tuple-element.63, ...), kind=kOutput, calls=%fused_computation.99 | convolution fusion | flops 29014784 | bytes 79616 | tf_op jit(solution)/shard_map/vmap(ts,ks->kt)/dot_general | solution.py:40
  65.9 1.1 fusion.81
  67.1 1.3 convolution_add_fusion.5
  68.5 5.3 %collective-permute-done.1 = f32[1,3,152]{2,1,0:T(4,128)S(1)} collective-permute-done((f32[1,3,152]{2,1,0:T(4,128)S(1)}, f32[1,3,152]{2,1,0:T(4,128)S(1)}, u32[]{:S(2)}, u32[]{:S(2)}) %collective-permute-start.1) | collective-permute-done | bytes 1856 | tf_op jit(solution)/shard_map/ppermute | solution.py:26
  74.3 4.9 %collective-permute-done.2 = f32[1,3,152]{2,1,0:T(4,128)S(1)} collective-permute-done((f32[1,3,152]{2,1,0:T(4,128)S(1)}, f32[1,3,152]{2,1,0:T(4,128)S(1)}, u32[]{:S(2)}, u32[]{:S(2)}) %collective-permute-start.2) | collective-permute-done | bytes 1856 | tf_op jit(solution)/shard_map/ppermute | solution.py:26
  79.3 0.3 dynamic_update_slice.27
  79.9 0.7 fusion.107
  80.7 0.8 fusion.73
  81.5 0.3 fusion.215
  81.8 0.4 fusion.198
  82.3 0.9 multiply_reduce_fusion
  83.2 0.5 convolution_bitcast_fusion
  83.7 8.1 %all-gather.7 = f32[8,3,152]{2,1,0:T(4,128)S(1)} all-gather(f32[1,3,152]{2,1,0:T(4,128)S(1)} %convolution_bitcast_fusion), channel_id=5, replica_groups=mesh['grp'=4,'dev'=8] {'dev'}, dimensions={0}, use_global_device_ids=true | all-gather | bytes 16416 | tf_op jit(solution)/shard_map/all_gather | solution.py:113
  92.0 0.2 convolution_bitcast_fusion.2
  92.2 0.1 broadcast_multiply_fusion.4
  92.3 13.2 %all-reduce.2 = f32[24]{0:T(128)S(1)} all-reduce(f32[24]{0:T(128)S(1)} %get-tuple-element.88), channel_id=6, replica_groups=mesh['grp'=4,'dev'=8] {'dev'}, use_global_device_ids=true, to_apply=%add.2 | all-reduce | flops 24 | bytes 192
  106.5 10.1 %all_gather.31 = f32[6,32,544]{2,0,1:T(8,128)S(1)} all-gather(f32[6,4,544]{2,0,1:T(8,128)S(1)} %copy.69), channel_id=1, replica_groups=mesh['grp'=4,'dev'=8] {'dev'}, dimensions={1}, use_global_device_ids=true | all-gather | bytes 470016 | tf_op jit(solution)/shard_map/all_gather | solution.py:101
  116.6 0.5 gather_fusion.2
  117.3 0.6 gather_fusion.3
  118.0 4.4 %fusion.18 = (f32[2,544]{1,0:T(2,128)S(1)}, f32[2,544]{1,0:T(2,128)S(1)}, f32[2,544]{1,0:T(2,128)S(1)}) fusion(f32[2,544]{1,0:T(2,128)S(1)} %bitcast.162, f32[2,544]{1,0:T(2,128)S(1)} %bitcast.171, f32[2,544]{1,0:T(2,128)S(1)} %bitcast.164, f32[2,544]{1,0:T(2,128)S(1)} %bitcast.158, f32[2,544]{1,0:T(2,128)S(1)} %bitcast.167, f32[2,544]{1,0:T(2,128)S(1)} %bitcast.165, ...), kind=kLoop, calls=%fused_computation.42 | loop fusion | flops 13609792 | bytes 52224 | tf_op jit(solution)/shard_map/vmap()/reduce_sum | solution.py:43
  122.5 0.3 multiply_dynamic-update-slice_fusion
  122.8 4.6 %fusion.61 = f32[3,2,544]{2,0,1:T(4,128)S(1)} fusion(f32[2,544]{1,0:T(2,128)S(1)} %bitcast.159, f32[2,544]{1,0:T(2,128)S(1)} %bitcast.168, f32[2,544]{1,0:T(2,128)S(1)} %bitcast.161, f32[2,544]{1,0:T(2,128)S(1)} %bitcast.170, f32[2,544]{1,0:T(2,128)S(1)} %bitcast.163, f32[2,544]{1,0:T(2,128)S(1)} %bitcast.172, f32[6,2,544]{2,0,1:T(8,128)S(1)} %select_bitcast_fusion, ...), kind=kOutput, calls=%fused_computation.97 | convolution fusion | flops 29014784 | bytes 79616 | tf_op jit(solution)/shard_map/vmap(ts,ks->kt)/dot_general | solution.py:40
  127.3 1.1 fusion.92
  128.5 1.3 convolution_add_fusion.4
  129.8 11.9 %all-reduce.3 = f32[12]{0:T(128)S(1)} all-reduce(f32[12]{0:T(128)S(1)} %multiply_dynamic-update-slice_fusion), channel_id=7, replica_groups=mesh['grp'=4,'dev'=8] {'grp'}, use_global_device_ids=true, to_apply=%add.3 | all-reduce | flops 12 | bytes 96
  141.9 5.3 %collective-permute-done.4 = f32[1,3,152]{2,1,0:T(4,128)S(1)} collective-permute-done((f32[1,3,152]{2,1,0:T(4,128)S(1)}, f32[1,3,152]{2,1,0:T(4,128)S(1)}, u32[]{:S(2)}, u32[]{:S(2)}) %collective-permute-start.4) | collective-permute-done | bytes 1856 | tf_op jit(solution)/shard_map/ppermute | solution.py:26
  147.7 4.9 %collective-permute-done.5 = f32[1,3,152]{2,1,0:T(4,128)S(1)} collective-permute-done((f32[1,3,152]{2,1,0:T(4,128)S(1)}, f32[1,3,152]{2,1,0:T(4,128)S(1)}, u32[]{:S(2)}, u32[]{:S(2)}) %collective-permute-start.5) | collective-permute-done | bytes 1856 | tf_op jit(solution)/shard_map/ppermute | solution.py:26
  153.1 0.7 fusion.118
  153.8 0.8 fusion.71
  154.7 0.3 fusion.216
  155.0 0.9 multiply_add_fusion
  (156 shorter events, 5.2 us)
Async XLA Ops:
  0.6 1.6 %copy-start = (f32[544,544]{1,0:T(8,128)S(1)}, f32[544,544]{1,0:T(8,128)}, u32[]{:S(2)}) copy-start(f32[544,544]{1,0:T(8,128)} %param.17) | copy-start | bytes 3551236
  0.6 16.2 %copy-start.11 = (u32[32]{0:T(128)S(1)}, u32[32]{0:T(128)}, u32[]{:S(2)}) copy-start(u32[32]{0:T(128)} %constant.118) | copy-start | bytes 388
  0.7 30.6 %copy-start.10 = (u32[32]{0:T(128)S(1)}, u32[32]{0:T(128)}, u32[]{:S(2)}) copy-start(u32[32]{0:T(128)} %constant.123) | copy-start | bytes 388
  0.7 3.2 %copy-start.1 = (f32[544,152]{0,1:T(8,128)S(1)}, f32[544,152]{0,1:T(8,128)}, u32[]{:S(2)}) copy-start(f32[544,152]{0,1:T(8,128)} %param.18) | copy-start | bytes 992260
  0.7 14.4 %copy-start.4 = (f32[152,152]{1,0:T(8,128)S(1)}, f32[152,152]{1,0:T(8,128)}, u32[]{:S(2)}) copy-start(f32[152,152]{1,0:T(8,128)} %param.20) | copy-start | bytes 277252
  0.7 16.2 %copy-start.9 = (s32[1,2]{1,0:T(1,128)S(1)}, s32[1,2]{1,0:T(1,128)}, u32[]{:S(2)}) copy-start(s32[1,2]{1,0:T(1,128)} %param.22) | copy-start | bytes 28
  0.7 42.8 %copy-start.6 = (f32[3,152]{1,0:T(4,128)S(1)}, f32[3,152]{1,0:T(4,128)}, u32[]{:S(2)}) copy-start(f32[3,152]{1,0:T(4,128)} %param.21) | copy-start | bytes 5476
  0.7 43.8 %copy-start.3 = (f32[3,4,544]{2,1,0:T(4,128)S(1)}, f32[3,4,544]{2,1,0:T(4,128)}, u32[]{:S(2)}) copy-start(f32[3,4,544]{2,1,0:T(4,128)} %param.15) | copy-start | bytes 78340
  3.8 51.0 %copy-start.7 = (s32[1,2]{1,0:T(1,128)S(1)}, s32[1,2]{1,0:T(1,128)}, u32[]{:S(2)}) copy-start(s32[1,2]{1,0:T(1,128)} %param.24) | copy-start | bytes 28
  3.8 51.0 %copy-start.8 = (s32[1,2]{1,0:T(1,128)S(1)}, s32[1,2]{1,0:T(1,128)}, u32[]{:S(2)}) copy-start(s32[1,2]{1,0:T(1,128)} %param.23) | copy-start | bytes 28
  15.2 53.1 %collective-permute-start = (f32[1,3,152]{2,1,0:T(4,128)S(1)}, f32[1,3,152]{2,1,0:T(4,128)S(1)}, u32[]{:S(2)}, u32[]{:S(2)}) collective-permute-start(f32[1,3,152]{2,1,0:T(4,128)S(1)} %convolution_bitcast_fusion.3), channel_id=1, source_target_pairs={{0,8},{8,16},{16,24},{24,0},{1,9},{9,17},{17,25},{25,1},{2,10},{10... | collective-permute-start | bytes 5480 | tf_op jit(solution)/shard_map/ppermute | solution.py:26
  68.4 5.5 %collective-permute-start.1 = (f32[1,3,152]{2,1,0:T(4,128)S(1)}, f32[1,3,152]{2,1,0:T(4,128)S(1)}, u32[]{:S(2)}, u32[]{:S(2)}) collective-permute-start(f32[1,3,152]{2,1,0:T(4,128)S(1)} %collective-permute-done), channel_id=1, source_target_pairs={{0,8},{8,16},{16,24},{24,0},{1,9},{9,17},{17,25},{25,1},{2,10},{10... | collective-permute-start | bytes 5480 | tf_op jit(solution)/shard_map/ppermute | solution.py:26
  73.8 5.4 %collective-permute-start.2 = (f32[1,3,152]{2,1,0:T(4,128)S(1)}, f32[1,3,152]{2,1,0:T(4,128)S(1)}, u32[]{:S(2)}, u32[]{:S(2)}) collective-permute-start(f32[1,3,152]{2,1,0:T(4,128)S(1)} %collective-permute-done.1), channel_id=1, source_target_pairs={{0,8},{8,16},{16,24},{24,0},{1,9},{9,17},{17,25},{25,1},{2,10},{10... | collective-permute-start | bytes 5480 | tf_op jit(solution)/shard_map/ppermute | solution.py:26
  79.7 1.8 %copy-start.2 = (f32[152,544]{1,0:T(8,128)S(1)}, f32[152,544]{1,0:T(8,128)}, u32[]{:S(2)}) copy-start(f32[152,544]{1,0:T(8,128)} %param.19) | copy-start | bytes 992260
  80.7 1.6 %copy-start.5 = (f32[3,544]{1,0:T(4,128)S(1)}, f32[3,544]{1,0:T(4,128)}, u32[]{:S(2)}) copy-start(f32[3,544]{1,0:T(4,128)} %param.16) | copy-start | bytes 19588
  92.1 49.7 %collective-permute-start.3 = (f32[1,3,152]{2,1,0:T(4,128)S(1)}, f32[1,3,152]{2,1,0:T(4,128)S(1)}, u32[]{:S(2)}, u32[]{:S(2)}) collective-permute-start(f32[1,3,152]{2,1,0:T(4,128)S(1)} %convolution_bitcast_fusion.2), channel_id=1, source_target_pairs={{0,8},{8,16},{16,24},{24,0},{1,9},{9,17},{17,25},{25,1},{2,10},{10... | collective-permute-start | bytes 5480 | tf_op jit(solution)/shard_map/ppermute | solution.py:26
  141.8 5.4 %collective-permute-start.4 = (f32[1,3,152]{2,1,0:T(4,128)S(1)}, f32[1,3,152]{2,1,0:T(4,128)S(1)}, u32[]{:S(2)}, u32[]{:S(2)}) collective-permute-start(f32[1,3,152]{2,1,0:T(4,128)S(1)} %collective-permute-done.3), channel_id=1, source_target_pairs={{0,8},{8,16},{16,24},{24,0},{1,9},{9,17},{17,25},{25,1},{2,10},{10... | collective-permute-start | bytes 5480 | tf_op jit(solution)/shard_map/ppermute | solution.py:26
  147.2 5.4 %collective-permute-start.5 = (f32[1,3,152]{2,1,0:T(4,128)S(1)}, f32[1,3,152]{2,1,0:T(4,128)S(1)}, u32[]{:S(2)}, u32[]{:S(2)}) collective-permute-start(f32[1,3,152]{2,1,0:T(4,128)S(1)} %collective-permute-done.4), channel_id=1, source_target_pairs={{0,8},{8,16},{16,24},{24,0},{1,9},{9,17},{17,25},{25,1},{2,10},{10... | collective-permute-start | bytes 5480 | tf_op jit(solution)/shard_map/ppermute | solution.py:26
